TPU v7x, 32 devices: a whole 2x2x4 slice. The times are simulated.
32 devices in a mesh: dp: 8 (over y, x, core), head: 4 (over z).
Axes of the slice: x: 2, y: 2, z: 4, core: 2. Of those that a mesh axis runs over, the one named last changes fastest.
Arguments:
- tokens: bfloat16 [16384, 1024], P(('dp', 'head')), may hold values from -6 to 6
- first_values: bfloat16 [16384, 1024], P('dp', 'head'), may hold values from -6 to 6
- mixer_in: float32 [3, 1024, 1024], P(None, 'dp', 'head'), may hold values from -0.1875 to 0.1875
- mixer_out: float32 [1024, 1024], P('head', 'dp'), may hold values from -0.75 to 0.75
- gate_up: float32 [2, 1024, 2816], P(None, 'dp', 'head'), may hold values from -0.1875 to 0.1875
- down_weight: float32 [2816, 1024], P('head', 'dp'), may hold values from -0.109375 to 0.109375
- norm_gains: float32 [2, 1024], P(None, 'dp'), may hold values from 0.5 to 1.5
- lengths: int32 [8], P('dp'), may hold values from 128 to 2048, as said below
- cotangent: bfloat16 [16384, 1024], P(('dp', 'head')), may hold values from -6 to 6
Outputs:
- block_out: bfloat16 [16384, 1024], P(('dp', 'head'))
- tokens_grad: float32 [16384, 1024], P(('dp', 'head'))
- first_grad: float32 [16384, 1024], P('dp', 'head')
- mixer_in_grad: float32 [3, 1024, 1024], P(None, 'dp', 'head')
- mixer_out_grad: float32 [1024, 1024], P('head', 'dp')
- gate_up_grad: float32 [2, 1024, 2816], P(None, 'dp', 'head')
- down_grad: float32 [2816, 1024], P('head', 'dp')
- gains_grad: float32 [2, 1024], P(None, 'dp')
Inputs may be any that keep to these rules, and one draw needn't show every extreme that they name: `lengths`: positions from a sequence's length on are padding; some sequence has exactly 2048 real tokens in every draw.
All inputs are finite; a program needn't handle non-finite values.
Results may differ from a plain program's by a relative error of at most 0.013.
The roundings to bfloat16 on the way count: a program that leaves them out, or rounds other values in their place, can miss the bound.
Values may be sent and summed in bfloat16 or wider, within the bound.
No kernel may reach another device: no remote copies, remote signals or barrier semaphores. Data moves between devices by JAX's collectives and lax.ppermute only.
A program may use at most 128 MiB of HBM per device.

v0:
```python
import jax
import jax.numpy as jnp
from jax import lax
from jax.sharding import PartitionSpec as P

HDIM = 64
SEQ = 2048
epsilon = 1e-05
far_below = -1e30
rope_base = 10000.0


def rope_tables(width):
    half = width // 2
    rates = rope_base ** (-jnp.arange(half, dtype=jnp.float32) * 2.0 / width)
    angles = jnp.arange(SEQ, dtype=jnp.float32)[:, None] * rates[None, :]
    return (jnp.cos(angles)[:, None, :], jnp.sin(angles)[:, None, :])


def rotate(field, cosine, sine, direction):
    half = field.shape[-1] // 2
    first = field[..., :half]
    second = field[..., half:]
    return jnp.concatenate(
        [first * cosine - direction * second * sine, second * cosine + direction * first * sine],
        axis=-1,
    )


def rms_parts(field, gain):
    factor = lax.rsqrt(jnp.mean(field * field, axis=-1, keepdims=True) + epsilon)
    unit = field * factor
    return (unit * gain, unit, factor)


def rms_back(normed_grad, unit, factor, gain):
    scaled = normed_grad * gain
    field_grad = factor * (scaled - unit * jnp.mean(scaled * unit, axis=-1, keepdims=True))
    return (field_grad, jnp.sum(normed_grad * unit, axis=0))


def to_items(rows, seqs_here, heads_here):
    return (
        rows.reshape(seqs_here, SEQ, heads_here, HDIM)
        .transpose(0, 2, 1, 3)
        .reshape(seqs_here * heads_here, SEQ, HDIM)
    )


def from_items(items, seqs_here, heads_here):
    return (
        items.reshape(seqs_here, heads_here, SEQ, HDIM)
        .transpose(0, 2, 1, 3)
        .reshape(seqs_here * SEQ, heads_here * HDIM)
    )


def block_scores(query_block, keys, rows, length):
    places = jnp.arange(SEQ)
    raw = jnp.einsum("qe,ke->qk", query_block, keys, preferred_element_type=jnp.float32)
    allowed = (places[None, :] <= rows[:, None]) & (places[None, :] < length)
    return jnp.where(allowed, raw * HDIM ** (-0.5), far_below)


def attend_item(item):
    query, keys, values, length = item
    block = min(512, SEQ)

    def one_block(number):
        start = number * block
        query_block = lax.dynamic_slice_in_dim(query, start, block, 0)
        rows = start + jnp.arange(block)
        scores = block_scores(query_block, keys, rows, length)
        peak = jnp.max(scores, axis=-1, keepdims=True)
        powers = jnp.exp(scores - peak)
        total = jnp.sum(powers, axis=-1, keepdims=True)
        probs = (powers / total).astype(jnp.bfloat16)
        result = (
            jnp.dot(probs, values, preferred_element_type=jnp.float32) * (rows < length)[:, None]
        )
        return (result.astype(jnp.bfloat16), (peak + jnp.log(total))[:, 0])

    results, log_total = lax.map(one_block, jnp.arange(SEQ // block))
    return (results.reshape(SEQ, HDIM), log_total.reshape(SEQ))


def attend_back(item):
    query, keys, values, length, log_total, out_grad = item
    block = min(512, SEQ)

    def one_block(carry, number):
        keys_grad, values_grad = carry
        start = number * block
        query_block = lax.dynamic_slice_in_dim(query, start, block, 0)
        grad_block = lax.dynamic_slice_in_dim(out_grad, start, block, 0)
        total_block = lax.dynamic_slice_in_dim(log_total, start, block, 0)
        rows = start + jnp.arange(block)
        scores = block_scores(query_block, keys, rows, length)
        probs = jnp.exp(scores - total_block[:, None])
        values_grad = values_grad + jnp.einsum(
            "qk,qe->ke", probs.astype(jnp.bfloat16), grad_block, preferred_element_type=jnp.float32
        )
        prob_grad = jnp.einsum("qe,ke->qk", grad_block, values, preferred_element_type=jnp.float32)
        offset = jnp.sum(prob_grad * probs, axis=-1, keepdims=True)
        raw_grad = (probs * (prob_grad - offset) * HDIM ** (-0.5)).astype(jnp.bfloat16)
        query_grad = jnp.dot(raw_grad, keys, preferred_element_type=jnp.float32)
        keys_grad = keys_grad + jnp.einsum(
            "qk,qe->ke", raw_grad, query_block, preferred_element_type=jnp.float32
        )
        return ((keys_grad, values_grad), query_grad)

    empty = jnp.zeros((SEQ, HDIM), jnp.float32)
    (keys_grad, values_grad), query_grads = lax.scan(
        one_block, (empty, empty), jnp.arange(SEQ // block)
    )
    return (query_grads.reshape(SEQ, HDIM), keys_grad, values_grad)


def shards(
    tokens, first_values, mixer_in, mixer_out, gate_up, down_weight, norm_gains, lengths, cotangent
):
    seqs_here = lengths.shape[0]
    group_rows = seqs_here * SEQ
    heads_here = mixer_in.shape[2] // HDIM
    cosine, sine = rope_tables(HDIM)
    places = jnp.arange(SEQ)
    valid_rows = (places[None, :] < lengths[:, None]).astype(jnp.float32).reshape(group_rows)
    head_lengths = jnp.repeat(lengths, heads_here)
    qkv_low = mixer_in.astype(jnp.bfloat16)
    proj_low = mixer_out.astype(jnp.bfloat16)
    gates_low = gate_up.astype(jnp.bfloat16)
    down_low = down_weight.astype(jnp.bfloat16)
    gain_low = norm_gains.astype(jnp.bfloat16)
    full = (
        lax.all_gather(qkv_low, "dp", axis=1, tiled=True),
        lax.all_gather(proj_low, "dp", axis=1, tiled=True),
        lax.all_gather(gates_low, "dp", axis=1, tiled=True),
        lax.all_gather(down_low, "dp", axis=1, tiled=True),
        lax.all_gather(gain_low, "dp", axis=1, tiled=True),
    )
    qkv_full, proj_full, gates_full, down_full, gain_full = full
    gain_first = gain_full[0].astype(jnp.float32)
    gain_second = gain_full[1].astype(jnp.float32)
    token_rows = tokens.astype(jnp.float32)
    normed_a, unit_a, factor_a = rms_parts(token_rows, gain_first)
    mixer_rows = lax.all_gather(normed_a.astype(jnp.bfloat16), "head", axis=0, tiled=True)
    mixed = jnp.einsum("td,kdc->ktc", mixer_rows, qkv_full, preferred_element_type=jnp.float32)
    shape_four = (seqs_here, SEQ, heads_here, HDIM)
    query = rotate(mixed[0].reshape(shape_four), cosine, sine, 1.0).astype(jnp.bfloat16)
    keys = rotate(mixed[1].reshape(shape_four), cosine, sine, 1.0).astype(jnp.bfloat16)
    values = (0.5 * mixed[2] + 0.5 * first_values.astype(jnp.float32)).astype(jnp.bfloat16)
    query_items = query.transpose(0, 2, 1, 3).reshape(seqs_here * heads_here, SEQ, HDIM)
    keys_items = keys.transpose(0, 2, 1, 3).reshape(seqs_here * heads_here, SEQ, HDIM)
    values_items = to_items(values, seqs_here, heads_here)
    attended_items, log_total = lax.map(
        attend_item, (query_items, keys_items, values_items, head_lengths)
    )
    attended = from_items(attended_items, seqs_here, heads_here)
    piece = attended
    branch_a = lax.psum_scatter(
        jnp.dot(piece, proj_full, preferred_element_type=jnp.float32),
        "head",
        scatter_dimension=0,
        tiled=True,
    )
    hidden_state = token_rows + branch_a
    normed_b, unit_b, factor_b = rms_parts(hidden_state, gain_second)
    feed_rows = lax.all_gather(normed_b.astype(jnp.bfloat16), "head", axis=0, tiled=True)
    gated = jnp.einsum("td,kdf->ktf", feed_rows, gates_full, preferred_element_type=jnp.float32)
    gate = gated[0]
    upward = gated[1]
    sigmoid_gate = jax.nn.sigmoid(gate)
    silu_gate = gate * sigmoid_gate
    inner = (silu_gate * upward).astype(jnp.bfloat16)
    piece = inner
    branch_b = lax.psum_scatter(
        jnp.dot(piece, down_full, preferred_element_type=jnp.float32).astype(jnp.bfloat16),
        "head",
        scatter_dimension=0,
        tiled=True,
    ).astype(jnp.float32)
    block_out = (hidden_state + branch_b).astype(jnp.bfloat16)
    back_full = (
        lax.all_gather(qkv_low, "dp", axis=1, tiled=True),
        lax.all_gather(proj_low, "dp", axis=1, tiled=True),
        lax.all_gather(gates_low, "dp", axis=1, tiled=True),
        lax.all_gather(down_low, "dp", axis=1, tiled=True),
        lax.all_gather(gain_low, "dp", axis=1, tiled=True),
    )
    qkv_back, proj_back, gates_back, down_back, gain_back = back_full
    piece = lax.all_gather(cotangent, "head", axis=0, tiled=True)
    down_sum = jnp.einsum("tf,td->fd", inner, piece, preferred_element_type=jnp.float32)
    rows_grad = jnp.einsum("td,fd->tf", piece, down_back, preferred_element_type=jnp.float32)
    inner_grad = rows_grad
    gate_grad = inner_grad * upward * sigmoid_gate * (1.0 + gate * (1.0 - sigmoid_gate))
    mlp_grad = jnp.stack([gate_grad, inner_grad * silu_gate]).astype(jnp.bfloat16)
    gates_part = jnp.einsum("td,ktf->kdf", feed_rows, mlp_grad, preferred_element_type=jnp.float32)
    piece = mlp_grad
    normed_b_grad = lax.psum_scatter(
        jnp.einsum("ktf,kdf->td", piece, gates_back, preferred_element_type=jnp.float32),
        "head",
        scatter_dimension=0,
        tiled=True,
    )
    state_part, gain_b_grad = rms_back(
        normed_b_grad, unit_b, factor_b, gain_back[1].astype(jnp.float32)
    )
    state_grad = cotangent.astype(jnp.float32) + state_part
    branch_grad = state_grad.astype(jnp.bfloat16)
    piece = lax.all_gather(branch_grad, "head", axis=0, tiled=True)
    proj_sum = jnp.einsum("tc,td->cd", attended, piece, preferred_element_type=jnp.float32)
    rows_grad = jnp.einsum("td,cd->tc", piece, proj_back, preferred_element_type=jnp.float32)
    attended_grad = rows_grad
    attended_grad = (valid_rows[:, None] * attended_grad).astype(jnp.bfloat16)
    grad_items = to_items(attended_grad, seqs_here, heads_here)
    query_grad, keys_grad, values_grad = lax.map(
        attend_back, (query_items, keys_items, values_items, head_lengths, log_total, grad_items)
    )
    values_mix_grad = from_items(values_grad, seqs_here, heads_here)
    first_grad = 0.5 * values_mix_grad
    query_rows = query_grad.reshape(seqs_here, heads_here, SEQ, HDIM).transpose(0, 2, 1, 3)
    keys_rows = keys_grad.reshape(seqs_here, heads_here, SEQ, HDIM).transpose(0, 2, 1, 3)
    query_back = rotate(query_rows, cosine, sine, -1.0).reshape(group_rows, heads_here * HDIM)
    keys_back = rotate(keys_rows, cosine, sine, -1.0).reshape(group_rows, heads_here * HDIM)
    mixed_grad = jnp.stack([query_back, keys_back, 0.5 * values_mix_grad]).astype(jnp.bfloat16)
    qkv_part = jnp.einsum("td,ktc->kdc", mixer_rows, mixed_grad, preferred_element_type=jnp.float32)
    piece = mixed_grad
    normed_a_grad = lax.psum_scatter(
        jnp.einsum("ktc,kdc->td", piece, qkv_back, preferred_element_type=jnp.float32).astype(
            jnp.bfloat16
        ),
        "head",
        scatter_dimension=0,
        tiled=True,
    ).astype(jnp.float32)
    token_part, gain_a_grad = rms_back(
        normed_a_grad, unit_a, factor_a, gain_back[0].astype(jnp.float32)
    )
    tokens_grad = state_grad + token_part
    gain_grads = jnp.stack([gain_a_grad, gain_b_grad])
    summed = (
        lax.psum_scatter(qkv_part, "dp", scatter_dimension=1, tiled=True),
        lax.psum_scatter(proj_sum, "dp", scatter_dimension=1, tiled=True),
        lax.psum_scatter(gates_part, "dp", scatter_dimension=1, tiled=True),
        lax.psum_scatter(down_sum, "dp", scatter_dimension=1, tiled=True),
        lax.psum_scatter(gain_grads, "dp", scatter_dimension=1, tiled=True),
    )
    gains_grad = lax.psum(summed[4], "head")
    return (
        block_out,
        tokens_grad,
        first_grad,
        summed[0],
        summed[1],
        summed[2],
        summed[3],
        gains_grad,
    )


def solution(mesh):
    return jax.shard_map(
        shards,
        mesh=mesh,
        in_specs=(
            P(("dp", "head"), None),
            P("dp", "head"),
            P(None, "dp", "head"),
            P("head", "dp"),
            P(None, "dp", "head"),
            P("head", "dp"),
            P(None, "dp"),
            P("dp"),
            P(("dp", "head"), None),
        ),
        out_specs=(
            P(("dp", "head"), None),
            P(("dp", "head"), None),
            P("dp", "head"),
            P(None, "dp", "head"),
            P("head", "dp"),
            P(None, "dp", "head"),
            P("head", "dp"),
            P(None, "dp"),
        ),
        check_vma=False,
    )
```

profile of v0, /device:TPU:0, one launch (start us, length us, event | category | flops | bytes accessed | tf_op | source)
XLA Modules:
  0.0 1471.1 jit_solution(9712456741320512277)
XLA Ops:
  7.2 1.9 copy.60
  9.9 10.2 all_gather.32
  25.0 12.0 all_gather.35
  39.8 83.2 %all-gather.8.cloned.1.call-done = bf16[2048,1024]{1,0:T(8,128)(2,1)} async-done(((bf16[512,1024]{1,0:T(8,128)(2,1)}), bf16[2048,1024]{1,0:T(8,128)(2,1)}) %all-gather.8.cloned.1.call-update) | async-done | bytes 4194320 | tf_op jit(solution)/shard_map/all_gather | solution.py:146
  123.0 5.7 fusion.29
  135.0 127.7 %while.54 = (s32[]{:T(128)}, bf16[4,2048,64]{1,2,0:T(8,128)(2,1)}, f32[4,2048]{1,0:T(4,128)S(1)}, bf16[4,2048,64]{2,1,0:T(8,128)(2,1)}, bf16[4,2048,64]{2,1,0:T(...) while((s32[]{:T(128)}, bf16[4,2048,64]{1,2,0:T(8,128)(2,1)}, ...), condition=%wide.region_6.7_spmd, body=%wide.region_1.6_spmd.sunk | while | flops 278990336 | bytes 16777708 | solution.py:155
  138.6 27.0 %while.57 = (s32[]{:T(128)}, bf16[4,512,64]{1,2,0:T(8,128)(2,1)S(1)}, f32[4,512]{1,0:T(4,128)S(1)}, s32[4]{0:T(128)S(1)}, s32[]{:T(128)}, /*index=5*/bf16[2048,6...) while((s32[]{:T(128)}, ...), condition=%wide.region_5.5_spmd, body=%wide.region_2.4_spmd.sunk | while | flops 278990336 | bytes 13598931 | solution.py:83
  141.2 2.3 fusion.119
  147.9 2.3 fusion.119
  154.6 2.3 fusion.119
  161.4 2.3 fusion.119
  170.5 27.0 %while.57 = (s32[]{:T(128)}, bf16[4,512,64]{1,2,0:T(8,128)(2,1)S(1)}, f32[4,512]{1,0:T(4,128)S(1)}, s32[4]{0:T(128)S(1)}, s32[]{:T(128)}, /*index=5*/bf16[2048,6...) while((s32[]{:T(128)}, ...), condition=%wide.region_5.5_spmd, body=%wide.region_2.4_spmd.sunk | while | flops 278990336 | bytes 13598931 | solution.py:83
  173.1 2.3 fusion.119
  179.8 2.3 fusion.119
  186.6 2.3 fusion.119
  193.3 2.3 fusion.119
  202.4 27.0 %while.57 = (s32[]{:T(128)}, bf16[4,512,64]{1,2,0:T(8,128)(2,1)S(1)}, f32[4,512]{1,0:T(4,128)S(1)}, s32[4]{0:T(128)S(1)}, s32[]{:T(128)}, /*index=5*/bf16[2048,6...) while((s32[]{:T(128)}, ...), condition=%wide.region_5.5_spmd, body=%wide.region_2.4_spmd.sunk | while | flops 278990336 | bytes 13598931 | solution.py:83
  205.0 2.3 fusion.119
  211.7 2.3 fusion.119
  218.5 2.3 fusion.119
  225.2 2.3 fusion.119
  234.3 27.0 %while.57 = (s32[]{:T(128)}, bf16[4,512,64]{1,2,0:T(8,128)(2,1)S(1)}, f32[4,512]{1,0:T(4,128)S(1)}, s32[4]{0:T(128)S(1)}, s32[]{:T(128)}, /*index=5*/bf16[2048,6...) while((s32[]{:T(128)}, ...), condition=%wide.region_5.5_spmd, body=%wide.region_2.4_spmd.sunk | while | flops 278990336 | bytes 13598931 | solution.py:83
  236.9 2.3 fusion.119
  243.7 2.3 fusion.119
  250.4 2.3 fusion.119
  257.2 2.3 fusion.119
  262.7 6.7 fusion.66
  271.4 141.2 %reduce-scatter.12.cloned.1.call-done = f32[512,1024]{1,0:T(8,128)} async-done(((f32[2048,1024]{1,0:T(8,128)}), f32[512,1024]{1,0:T(8,128)}) %reduce-scatter.12.cloned.1.call-update) | async-done | bytes 2097168 | tf_op jit(solution)/shard_map/reduce_scatter | solution.py:160
  412.6 1.9 multiply_reduce_fusion.3
  417.9 29.4 %all-gather.14.cloned.1.call-done = bf16[2,1024,704]{1,2,0:T(8,128)(2,1)} async-done(((bf16[2,128,704]{1,2,0:T(8,128)(2,1)}), bf16[2,1024,704]{1,2,0:T(8,128)(2,1)}) %all-gather.14.cloned.1.call-update) | async-done | bytes 2883600 | tf_op jit(solution)/shard_map/all_gather | solution.py:137
  447.3 82.8 %all-gather.12.cloned.1.call-done = bf16[2048,1024]{1,0:T(8,128)(2,1)} async-done(((bf16[512,1024]{1,0:T(8,128)(2,1)}), bf16[2048,1024]{1,0:T(8,128)(2,1)}) %all-gather.12.cloned.1.call-update) | async-done | bytes 4194320 | tf_op jit(solution)/shard_map/all_gather | solution.py:168
  530.1 11.5 convolution_bitcast_fusion.1
  541.6 14.7 all-gather.16.cloned.1.call-done
  556.2 82.4 %all-gather.18.cloned.1.call-done = bf16[2048,1024]{1,0:T(8,128)(2,1)} async-done(((bf16[512,1024]{1,0:T(8,128)(2,1)}), bf16[2048,1024]{1,0:T(8,128)(2,1)}) %all-gather.18.cloned.1.call-update) | async-done | bytes 4194320 | tf_op jit(solution)/shard_map/all_gather | solution.py:191
  638.6 11.3 fusion.37
  652.5 9.0 convolution_bitcast_fusion.2
  661.5 143.1 %reduce-scatter.16.cloned.1.call-done = f32[512,1024]{1,0:T(8,128)} async-done(((f32[2048,1024]{1,0:T(8,128)}), f32[512,1024]{1,0:T(8,128)}) %reduce-scatter.16.cloned.1.call-update) | async-done | bytes 2097168 | tf_op jit(solution)/shard_map/reduce_scatter | solution.py:199
  804.6 2.9 multiply_reduce_fusion.1
  809.5 81.4 %all-gather.20.cloned.1.call-done = bf16[2048,1024]{1,0:T(8,128)(2,1)} async-done(((bf16[512,1024]{1,0:T(8,128)(2,1)}), bf16[2048,1024]{1,0:T(8,128)(2,1)}) %all-gather.20.cloned.1.call-update) | async-done | bytes 4194320 | tf_op jit(solution)/shard_map/all_gather | solution.py:210
  890.9 3.6 fusion.38
  896.3 154.4 %while.56 = (s32[]{:T(128)}, f32[4,2048,64]{1,2,0:T(8,128)}, f32[4,2048,64]{1,2,0:T(8,128)}, f32[4,2048,64]{1,2,0:T(8,128)}, bf16[4,2048,64]{2,1,0:T(8,128)(2,1)...) while((s32[]{:T(128)}, f32[4,2048,64]{1,2,0:T(8,128)}, ...), condition=%wide.region_16.17_spmd, body=%wide.region_12.16_spmd.sunk | while | flops 684197888 | bytes 42895948 | solution.py:216
  901.3 30.0 %while.58 = (s32[]{:T(128)}, f32[2048,64]{0,1:T(8,128)S(1)}, f32[2048,64]{0,1:T(8,128)S(1)}, f32[4,512,64]{1,2,0:T(8,128)}, s32[4]{0:T(128)S(1)}, /*index=5*/s32...) while((s32[]{:T(128)}, f32[2048,64]{0,1:T(8,128)S(1)}, ...), condition=%wide.region_15.15_spmd.clone, body=%wide.region_13.14_spmd.clone.sunk | while | flops 684197888 | bytes 35539192 | solution.py:113
  939.9 30.0 %while.58 = (s32[]{:T(128)}, f32[2048,64]{0,1:T(8,128)S(1)}, f32[2048,64]{0,1:T(8,128)S(1)}, f32[4,512,64]{1,2,0:T(8,128)}, s32[4]{0:T(128)S(1)}, /*index=5*/s32...) while((s32[]{:T(128)}, f32[2048,64]{0,1:T(8,128)S(1)}, ...), condition=%wide.region_15.15_spmd.clone, body=%wide.region_13.14_spmd.clone.sunk | while | flops 684197888 | bytes 35539192 | solution.py:113
  978.5 30.0 %while.58 = (s32[]{:T(128)}, f32[2048,64]{0,1:T(8,128)S(1)}, f32[2048,64]{0,1:T(8,128)S(1)}, f32[4,512,64]{1,2,0:T(8,128)}, s32[4]{0:T(128)S(1)}, /*index=5*/s32...) while((s32[]{:T(128)}, f32[2048,64]{0,1:T(8,128)S(1)}, ...), condition=%wide.region_15.15_spmd.clone, body=%wide.region_13.14_spmd.clone.sunk | while | flops 684197888 | bytes 35539192 | solution.py:113
  1017.1 30.0 %while.58 = (s32[]{:T(128)}, f32[2048,64]{0,1:T(8,128)S(1)}, f32[2048,64]{0,1:T(8,128)S(1)}, f32[4,512,64]{1,2,0:T(8,128)}, s32[4]{0:T(128)S(1)}, /*index=5*/s32...) while((s32[]{:T(128)}, f32[2048,64]{0,1:T(8,128)S(1)}, ...), condition=%wide.region_15.15_spmd.clone, body=%wide.region_13.14_spmd.clone.sunk | while | flops 684197888 | bytes 35539192 | solution.py:113
  1050.7 3.9 subtract_convert_fusion.1
  1062.3 7.1 bitcast_convert_fusion
  1070.7 7.4 fusion.52
  1079.5 6.9 convolution_convert_fusion
  1086.5 58.5 %reduce-scatter.18.cloned.1.call-done = bf16[512,1024]{1,0:T(8,128)(2,1)} async-done(((bf16[2048,1024]{1,0:T(8,128)(2,1)}), bf16[512,1024]{1,0:T(8,128)(2,1)}) %reduce-scatter.18.cloned.1.call-update) | async-done | bytes 1048592 | tf_op jit(solution)/shard_map/reduce_scatter | solution.py:228
  1144.9 2.0 fusion.47
  1148.1 7.8 fusion.68
  1156.0 11.5 fusion.39
  1168.7 4.4 fusion.67
  1173.2 3.0 copy.77
  1176.2 19.3 %reduce-scatter.20.cloned.1.call-done = f32[3,128,256]{1,2,0:T(8,128)} async-done(((f32[3,1024,256]{1,2,0:T(8,128)}), f32[3,128,256]{1,2,0:T(8,128)}) %reduce-scatter.20.cloned.1.call-update) | async-done | bytes 393232 | tf_op jit(solution)/shard_map/reduce_scatter | solution.py:242
  1195.5 1.9 copy.78
  1197.4 77.0 %reduce-scatter.14.cloned.1.call-done = bf16[512,1024]{1,0:T(8,128)(2,1)} async-done(((bf16[2048,1024]{1,0:T(8,128)(2,1)}), bf16[512,1024]{1,0:T(8,128)(2,1)}) %reduce-scatter.14.cloned.1.call-update) | async-done | bytes 1048592 | tf_op jit(solution)/shard_map/reduce_scatter | solution.py:176
  1274.5 4.3 fusion.44
  1278.7 33.8 %reduce-scatter.28.cloned.1.call-done = f32[128,2]{1,0:T(8,128)} async-done(((f32[1024,2]{1,0:T(8,128)}), f32[128,2]{1,0:T(8,128)}) %reduce-scatter.28.cloned.1.call-update) | async-done | bytes 1040
  1313.4 12.2 psum.7
  1325.6 35.6 %reduce-scatter.26.cloned.1.call-done = f32[704,128]{1,0:T(8,128)} async-done(((f32[704,1024]{1,0:T(8,128)}), f32[704,128]{1,0:T(8,128)}) %reduce-scatter.26.cloned.1.call-update) | async-done | bytes 360464 | tf_op jit(solution)/shard_map/reduce_scatter | solution.py:245
  1361.2 63.3 %reduce-scatter.24.cloned.1.call-done = f32[2,128,704]{1,2,0:T(8,128)} async-done(((f32[2,1024,704]{1,2,0:T(8,128)}), f32[2,128,704]{1,2,0:T(8,128)}) %reduce-scatter.24.cloned.1.call-update) | async-done | bytes 720912 | tf_op jit(solution)/shard_map/reduce_scatter | solution.py:244
  1424.5 39.6 %reduce-scatter.22.cloned.1.call-done = f32[256,128]{1,0:T(8,128)} async-done(((f32[256,1024]{1,0:T(8,128)}), f32[256,128]{1,0:T(8,128)}) %reduce-scatter.22.cloned.1.call-update) | async-done | bytes 131088 | tf_op jit(solution)/shard_map/reduce_scatter | solution.py:243
  (529 shorter events, 262.1 us)
Async XLA Ops:
  7.2 15.1 %copy-start.2 = (bf16[512,1024]{1,0:T(8,128)(2,1)S(1)}, bf16[512,1024]{1,0:T(8,128)(2,1)}, u32[]{:S(2)}) copy-start(bf16[512,1024]{1,0:T(8,128)(2,1)} %param.17) | copy-start | bytes 3145732
  7.2 32.6 %all-gather.10.cloned.1.call-start = ((), (), s32[]{:S(2)}) async-start(), calls=%async_computation.10 | async-start | bytes 1769472 | tf_op jit(solution)/shard_map/all_gather | solution.py:135
  9.1 113.8 %all-gather.8.cloned.1.call-start = ((), (), s32[]{:S(2)}) async-start(), calls=%async_computation.9 | async-start | bytes 5242880 | tf_op jit(solution)/shard_map/all_gather | solution.py:146
  20.1 4.3 copy-start.18
  20.1 4.3 copy-start.12
  21.7 2.6 copy-start.25
  22.3 2.0 copy-start.21
  23.6 389.0 %reduce-scatter.12.cloned.1.call-start = ((), (), s32[]{:S(2)}) async-start(), calls=%async_computation.11 | async-start | bytes 10485760 | tf_op jit(solution)/shard_map/reduce_scatter | solution.py:160
  38.8 90.7 %copy-start.8 = (f32[2048,32]{0,1:T(8,128)}, f32[2048,32]{0,1:T(8,128)S(1)}, u32[]{:S(2)}) copy-start(f32[2048,32]{0,1:T(8,128)S(1)} %get-tuple-element.429) | copy-start | bytes 786436
  262.7 6.7 copy-start.5
  269.4 1.1 copy-start.16
  269.4 143.2 %copy-start.3 = (bf16[512,1024]{1,0:T(8,128)(2,1)S(1)}, bf16[512,1024]{1,0:T(8,128)(2,1)}, u32[]{:S(2)}) copy-start(bf16[512,1024]{1,0:T(8,128)(2,1)} %param.17) | copy-start | bytes 3145732
  269.4 177.9 %all-gather.14.cloned.1.call-start = ((), (), s32[]{:S(2)}) async-start(), calls=%async_computation.13 | async-start | bytes 3244032 | tf_op jit(solution)/shard_map/all_gather | solution.py:137
  271.3 143.2 %copy-start.19 = (f32[1,1024]{1,0:T(1,128)S(1)}, f32[1,1024]{1,0:T(1,128)}, u32[]{:S(2)}) copy-start(f32[1,1024]{1,0:T(1,128)} %get-tuple-element.425) | copy-start | bytes 12292
  271.3 258.8 %all-gather.12.cloned.1.call-start = ((), (), s32[]{:S(2)}) async-start(), calls=%async_computation.12 | async-start | bytes 5242880 | tf_op jit(solution)/shard_map/all_gather | solution.py:168
  414.5 393.0 %copy-start = (f32[512,1024]{1,0:T(8,128)}, f32[512,1024]{1,0:T(8,128)S(1)}, u32[]{:S(2)}) copy-start(f32[512,1024]{1,0:T(8,128)S(1)} %get-tuple-element.395) | copy-start | bytes 6291460
  414.5 393.0 %copy-start.23 = (f32[512]{0:T(512)}, f32[512]{0:T(512)S(1)}, u32[]{:S(2)}) copy-start(f32[512]{0:T(512)S(1)} %add_rsqrt_fusion) | copy-start | bytes 6148
  414.6 1.3 copy-start.17
  415.8 140.4 %all-gather.16.cloned.1.call-start = ((), (), s32[]{:S(2)}) async-start(), calls=%async_computation.14 | async-start | bytes 1622016 | tf_op jit(solution)/shard_map/all_gather | solution.py:138
  416.6 222.0 %all-gather.18.cloned.1.call-start = ((), (), s32[]{:S(2)}) async-start(), calls=%async_computation.16 | async-start | bytes 5242880 | tf_op jit(solution)/shard_map/all_gather | solution.py:191
  417.3 387.3 %reduce-scatter.16.cloned.1.call-start = ((), (), s32[]{:S(2)}) async-start(), calls=%async_computation.17 | async-start | bytes 10485760 | tf_op jit(solution)/shard_map/reduce_scatter | solution.py:199
  638.6 13.9 copy-start.30
  649.9 1.5 copy-start.32
  649.9 2.5 copy-start.33
  661.5 146.1 %copy-start.7 = (bf16[512,1024]{1,0:T(8,128)(2,1)S(1)}, bf16[512,1024]{1,0:T(8,128)(2,1)}, u32[]{:S(2)}) copy-start(bf16[512,1024]{1,0:T(8,128)(2,1)} %param.25) | copy-start | bytes 3145732
  661.5 229.4 %all-gather.20.cloned.1.call-start = ((), (), s32[]{:S(2)}) async-start(), calls=%async_computation.18 | async-start | bytes 5242880 | tf_op jit(solution)/shard_map/all_gather | solution.py:210
  804.6 2.9 copy-start.6
  807.6 1.6 copy-start.27
  809.2 335.7 %reduce-scatter.18.cloned.1.call-start = ((), (), s32[]{:S(2)}) async-start(), calls=%async_computation.19 | async-start | bytes 5242880 | tf_op jit(solution)/shard_map/reduce_scatter | solution.py:228
  896.3 154.5 %copy-start.9 = (f32[2048,32]{0,1:T(8,128)S(1)}, f32[2048,32]{0,1:T(8,128)}, u32[]{:S(2)}) copy-start(f32[2048,32]{0,1:T(8,128)} %copy-done.8) | copy-start | bytes 786436
  1056.0 2.8 copy-start.10
  1060.4 1.3 copy-start.13
  1060.4 1.9 copy-start.14
  1069.5 1.2 copy-start.15
  1069.5 126.0 %reduce-scatter.20.cloned.1.call-start = ((), (), s32[]{:S(2)}) async-start(), calls=%async_computation.20 | async-start | bytes 3538944 | tf_op jit(solution)/shard_map/reduce_scatter | solution.py:242
  1078.1 1.4 copy-start.31
  1078.2 196.3 %reduce-scatter.14.cloned.1.call-start = ((), (), s32[]{:S(2)}) async-start(), calls=%async_computation.15 | async-start | bytes 5242880 | tf_op jit(solution)/shard_map/reduce_scatter | solution.py:176
  1086.4 58.5 %copy-start.4 = (bf16[512,1024]{1,0:T(8,128)(2,1)S(1)}, bf16[512,1024]{1,0:T(8,128)(2,1)}, u32[]{:S(2)}) copy-start(bf16[512,1024]{1,0:T(8,128)(2,1)} %param.17) | copy-start | bytes 3145732
  1086.4 58.5 %copy-start.22 = (f32[1,1024]{1,0:T(1,128)S(1)}, f32[1,1024]{1,0:T(1,128)}, u32[]{:S(2)}) copy-start(f32[1,1024]{1,0:T(1,128)} %copy-done.21) | copy-start | bytes 12292
  1086.4 58.5 %copy-start.26 = (f32[512]{0:T(512)S(1)}, f32[512]{0:T(512)}, u32[]{:S(2)}) copy-start(f32[512]{0:T(512)} %copy-done.25) | copy-start | bytes 6148
  1086.4 60.6 %copy-start.29 = (f32[1024]{0:T(1024)S(1)}, f32[1024]{0:T(1024)}, u32[]{:S(2)}) copy-start(f32[1024]{0:T(1024)} %get-tuple-element.318) | copy-start | bytes 12292
  1086.4 226.1 %reduce-scatter.28.cloned.1.call-start = ((), (), s32[]{:S(2)}) async-start(), calls=%async_computation.24 | async-start | bytes 589824
  1148.1 213.1 %reduce-scatter.26.cloned.1.call-start = ((), (), s32[]{:S(2)}) async-start(), calls=%async_computation.23 | async-start | bytes 3244032 | tf_op jit(solution)/shard_map/reduce_scatter | solution.py:245
  1155.9 268.6 %reduce-scatter.24.cloned.1.call-start = ((), (), s32[]{:S(2)}) async-start(), calls=%async_computation.22 | async-start | bytes 6488064 | tf_op jit(solution)/shard_map/reduce_scatter | solution.py:244
  1167.5 1.2 copy-start.11
  1167.5 296.6 %reduce-scatter.22.cloned.1.call-start = ((), (), s32[]{:S(2)}) async-start(), calls=%async_computation.21 | async-start | bytes 1179648 | tf_op jit(solution)/shard_map/reduce_scatter | solution.py:243
  1173.2 101.3 %copy-start.1 = (f32[512,1024]{1,0:T(8,128)S(1)}, f32[512,1024]{1,0:T(8,128)}, u32[]{:S(2)}) copy-start(f32[512,1024]{1,0:T(8,128)} %copy-done) | copy-start | bytes 6291460
  1173.2 101.3 %copy-start.20 = (f32[1,1024]{1,0:T(1,128)S(1)}, f32[1,1024]{1,0:T(1,128)}, u32[]{:S(2)}) copy-start(f32[1,1024]{1,0:T(1,128)} %get-tuple-element.425) | copy-start | bytes 12292
  1173.2 101.3 %copy-start.24 = (f32[512]{0:T(512)S(1)}, f32[512]{0:T(512)}, u32[]{:S(2)}) copy-start(f32[512]{0:T(512)} %copy-done.23) | copy-start | bytes 6148
  1173.2 101.2 %copy-start.28 = (f32[512]{0:T(512)S(1)}, f32[512]{0:T(512)}, u32[]{:S(2)}) copy-start(f32[512]{0:T(512)} %copy-done.27) | copy-start | bytes 6148
Sparse Core Ops, SparseCore 0:
  10.5 29.2 all-gather.9
  41.9 80.9 all-gather.7
  269.5 143.0 reduce-scatter.11
  414.9 32.3 all-gather.13
  449.3 80.7 all-gather.11
  532.4 23.8 all-gather.15
  557.8 80.7 all-gather.17
  661.6 143.0 reduce-scatter.15
  809.4 81.4 all-gather.19
  1069.6 75.2 reduce-scatter.17
  1148.7 46.7 reduce-scatter.19
  1197.7 76.7 reduce-scatter.13
  1277.8 34.6 reduce-scatter.27
  1316.3 44.8 reduce-scatter.25
  1365.5 58.9 reduce-scatter.23
  1428.1 35.9 reduce-scatter.21
where the time goes:
time: 1480 us; the launch traced here: 1470 us
  waiting for transfers between devices  987 us (67%)
  matrix products  226 us (15%)
  local copies, waits for them, and re-layouts  102 us (7%)
  other arithmetic  81.1 us (5%)
  blocking collectives  34.4 us (2%)
  loops' own time  22.6 us (2%)
  between operations  15.4 us (1%)
    reduce_scatter x1, waiting for transfers between devices, shards(): lax.psum_scatter(jnp.einsum('ktf,kdf->td', piece, gates_back, preferred_e...  143 us
    reduce_scatter x1, waiting for transfers between devices, shards(): lax.psum_scatter(jnp.dot(piece, proj_full, preferred_element_type=jnp.flo...  141 us
    all_gather x1, waiting for transfers between devices, shards(): lax.all_gather(normed_a.astype(jnp.bfloat16), 'head', axis=0, tiled=True)  83.2 us
    all_gather x1, waiting for transfers between devices, shards(): lax.all_gather(normed_b.astype(jnp.bfloat16), 'head', axis=0, tiled=True)  82.8 us
    all_gather x1, waiting for transfers between devices, shards(): piece = lax.all_gather(cotangent, 'head', axis=0, tiled=True)  82.4 us
    all_gather x1, waiting for transfers between devices, shards(): piece = lax.all_gather(branch_grad, 'head', axis=0, tiled=True)  81.4 us
    reduce_scatter x1, waiting for transfers between devices, shards(): lax.psum_scatter(jnp.dot(piece, down_full, preferred_element_type=jnp.flo...  77 us
    reduce_scatter x1, waiting for transfers between devices, shards(): lax.psum_scatter(gates_part, 'dp', scatter_dimension=1, tiled=True)  63.3 us
  transfers between devices with their start and end apart: 16, of which 16 were waited for; matrix products, arithmetic and copies ran while one was open for 5% of the time, Pallas kernels for 0%

commit v1 on v0

--- a/solution.py
+++ b/solution.py
@@ -188,7 +188,12 @@
         lax.all_gather(gain_low, "dp", axis=1, tiled=True),
     )
     qkv_back, proj_back, gates_back, down_back, gain_back = back_full
-    piece = lax.all_gather(cotangent, "head", axis=0, tiled=True)
+    ring = [cotangent]
+    for hop in range(3):
+        ring.append(lax.ppermute(ring[-1], "head", [(dev, (dev + 1) % 4) for dev in range(4)]))
+    piece = jnp.roll(
+        jnp.concatenate(ring[::-1], axis=0), (lax.axis_index("head") + 1) * ring[0].shape[0], axis=0
+    )
     down_sum = jnp.einsum("tf,td->fd", inner, piece, preferred_element_type=jnp.float32)
     rows_grad = jnp.einsum("td,fd->tf", piece, down_back, preferred_element_type=jnp.float32)
     inner_grad = rows_grad

time: 1480 us -> 1430 us (0.966)
  waiting for transfers between devices: 987 us -> 908 us
  local copies, waits for them, and re-layouts: 102 us -> 117 us
    ppermute x0 -> x3, waiting for transfers between devices: none -> 104 us  [shards(): lax.ppermute(ring[-1], 'head', [(dev, (dev + 1) % 4) for dev in range(4)])]
    all_gather x1 -> x0, waiting for transfers between devices: 82.4 us -> none  [shards(): piece = lax.all_gather(cotangent, 'head', axis=0, tiled=True)]
    all_gather x1, waiting for transfers between devices: 82.8 us -> 14 us  [shards(): lax.all_gather(normed_b.astype(jnp.bfloat16), 'head', axis=0, tiled=True)]
    all_gather x1, waiting for transfers between devices: 29.4 us -> 0.01 us  [shards(): lax.all_gather(gates_low, 'dp', axis=1, tiled=True)]
    unnamed x74 -> x81, local copies, waits for them, and re-layouts: 16.9 us -> 31.1 us
    unnamed x17 -> x16, waiting for transfers between devices: 34.7 us -> 33.9 us
  transfers between devices with their start and end apart: 16 -> 18, of which waited for: 16 -> 16; matrix products, arithmetic and copies ran while one was open for 5% -> 6% of each run, Pallas kernels for 0% -> 0%
where the time goes in v1:
time: 1430 us; the launch traced here: 1420 us
  waiting for transfers between devices  908 us (63%)
  matrix products  227 us (16%)
  local copies, waits for them, and re-layouts  117 us (8%)
  other arithmetic  82 us (6%)
  blocking collectives  35.4 us (2%)
  loops' own time  21.9 us (2%)
  between operations  15.4 us (1%)
    reduce_scatter x1, waiting for transfers between devices, shards(): lax.psum_scatter(jnp.einsum('ktf,kdf->td', piece, gates_back, preferred_e...  145 us
    reduce_scatter x1, waiting for transfers between devices, shards(): lax.psum_scatter(jnp.dot(piece, proj_full, preferred_element_type=jnp.flo...  141 us
    ppermute x3, waiting for transfers between devices, shards(): lax.ppermute(ring[-1], 'head', [(dev, (dev + 1) % 4) for dev in range(4)])  104 us
    all_gather x1, waiting for transfers between devices, shards(): lax.all_gather(normed_a.astype(jnp.bfloat16), 'head', axis=0, tiled=True)  81.9 us
    all_gather x1, waiting for transfers between devices, shards(): piece = lax.all_gather(branch_grad, 'head', axis=0, tiled=True)  81.4 us
    reduce_scatter x1, waiting for transfers between devices, shards(): lax.psum_scatter(jnp.dot(piece, down_full, preferred_element_type=jnp.flo...  77.2 us
    reduce_scatter x1, waiting for transfers between devices, shards(): lax.psum_scatter(gates_part, 'dp', scatter_dimension=1, tiled=True)  63.3 us
    dot_general x32, matrix products, block_scores(): jnp.einsum('qe,ke->qk', query_block, keys, preferred_element_type=jnp.flo...  61.9 us
  transfers between devices with their start and end apart: 18, of which 16 were waited for; matrix products, arithmetic and copies ran while one was open for 6% of the time, Pallas kernels for 0%

profile of v1, /device:TPU:0, one launch (start us, length us, event | category | flops | bytes accessed | tf_op | source)
XLA Modules:
  0.0 1419.0 jit_solution(10024100544367169658)
XLA Ops:
  9.9 10.2 all_gather.29
  22.8 2.5 fusion.49
  26.8 13.0 all_gather.32
  41.6 81.9 %all-gather.7.cloned.1.call-done = bf16[2048,1024]{1,0:T(8,128)(2,1)} async-done(((bf16[512,1024]{1,0:T(8,128)(2,1)}), bf16[2048,1024]{1,0:T(8,128)(2,1)}) %all-gather.7.cloned.1.call-update) | async-done | bytes 4194320 | tf_op jit(solution)/shard_map/all_gather | solution.py:146
  123.4 5.7 fusion.29
  135.4 127.7 %while.54 = (s32[]{:T(128)}, bf16[4,2048,64]{1,2,0:T(8,128)(2,1)}, f32[4,2048]{1,0:T(4,128)S(1)}, bf16[4,2048,64]{2,1,0:T(8,128)(2,1)}, bf16[4,2048,64]{2,1,0:T(...) while((s32[]{:T(128)}, bf16[4,2048,64]{1,2,0:T(8,128)(2,1)}, ...), condition=%wide.region_6.7_spmd, body=%wide.region_1.6_spmd.sunk | while | flops 278990336 | bytes 16777708 | solution.py:155
  139.0 27.0 %while.57 = (s32[]{:T(128)}, bf16[4,512,64]{1,2,0:T(8,128)(2,1)S(1)}, f32[4,512]{1,0:T(4,128)S(1)}, s32[4]{0:T(128)S(1)}, s32[]{:T(128)}, /*index=5*/bf16[2048,6...) while((s32[]{:T(128)}, ...), condition=%wide.region_5.5_spmd, body=%wide.region_2.4_spmd.sunk | while | flops 278990336 | bytes 13598931 | solution.py:83
  141.6 2.3 fusion.124
  148.3 2.3 fusion.124
  155.1 2.3 fusion.124
  161.8 2.3 fusion.124
  170.9 27.0 %while.57 = (s32[]{:T(128)}, bf16[4,512,64]{1,2,0:T(8,128)(2,1)S(1)}, f32[4,512]{1,0:T(4,128)S(1)}, s32[4]{0:T(128)S(1)}, s32[]{:T(128)}, /*index=5*/bf16[2048,6...) while((s32[]{:T(128)}, ...), condition=%wide.region_5.5_spmd, body=%wide.region_2.4_spmd.sunk | while | flops 278990336 | bytes 13598931 | solution.py:83
  173.5 2.3 fusion.124
  180.3 2.3 fusion.124
  187.0 2.3 fusion.124
  193.8 2.3 fusion.124
  202.9 27.0 %while.57 = (s32[]{:T(128)}, bf16[4,512,64]{1,2,0:T(8,128)(2,1)S(1)}, f32[4,512]{1,0:T(4,128)S(1)}, s32[4]{0:T(128)S(1)}, s32[]{:T(128)}, /*index=5*/bf16[2048,6...) while((s32[]{:T(128)}, ...), condition=%wide.region_5.5_spmd, body=%wide.region_2.4_spmd.sunk | while | flops 278990336 | bytes 13598931 | solution.py:83
  205.4 2.3 fusion.124
  212.2 2.3 fusion.124
  218.9 2.3 fusion.124
  225.7 2.3 fusion.124
  234.8 27.0 %while.57 = (s32[]{:T(128)}, bf16[4,512,64]{1,2,0:T(8,128)(2,1)S(1)}, f32[4,512]{1,0:T(4,128)S(1)}, s32[4]{0:T(128)S(1)}, s32[]{:T(128)}, /*index=5*/bf16[2048,6...) while((s32[]{:T(128)}, ...), condition=%wide.region_5.5_spmd, body=%wide.region_2.4_spmd.sunk | while | flops 278990336 | bytes 13598931 | solution.py:83
  237.4 2.3 fusion.124
  244.1 2.3 fusion.124
  250.9 2.3 fusion.124
  257.6 2.3 fusion.124
  263.1 6.7 fusion.74
  271.8 141.2 %reduce-scatter.12.cloned.1.call-done = f32[512,1024]{1,0:T(8,128)} async-done(((f32[2048,1024]{1,0:T(8,128)}), f32[512,1024]{1,0:T(8,128)}) %reduce-scatter.12.cloned.1.call-update) | async-done | bytes 2097168 | tf_op jit(solution)/shard_map/reduce_scatter | solution.py:160
  418.1 25.3 %collective-permute-done = bf16[512,1024]{1,0:T(8,128)(2,1)S(1)} collective-permute-done((bf16[512,1024]{1,0:T(8,128)(2,1)S(1)}, bf16[512,1024]{1,0:T(8,128)(2,1)S(1)}, u32[]{:S(2)}, u32[]{:S(2)}) %collective-permute-start) | collective-permute-done | bytes 1048608 | tf_op jit(solution)/shard_map/ppermute | solution.py:193
  445.0 36.1 %collective-permute-done.1 = bf16[512,1024]{1,0:T(8,128)(2,1)} collective-permute-done((bf16[512,1024]{1,0:T(8,128)(2,1)S(1)}, bf16[512,1024]{1,0:T(8,128)(2,1)}, u32[]{:S(2)}, u32[]{:S(2)}) %collective-permute-start.1) | collective-permute-done | bytes 1048608 | tf_op jit(solution)/shard_map/ppermute | solution.py:193
  481.1 9.7 collective-permute-start.2
  491.6 42.1 %collective-permute-done.2 = bf16[512,1024]{1,0:T(8,128)(2,1)} collective-permute-done((bf16[512,1024]{1,0:T(8,128)(2,1)}, bf16[512,1024]{1,0:T(8,128)(2,1)}, u32[]{:S(2)}, u32[]{:S(2)}) %collective-permute-start.2) | collective-permute-done | bytes 1048608 | tf_op jit(solution)/shard_map/ppermute | solution.py:193
  533.7 2.3 constant_dynamic-update-slice_fusion.9
  547.1 14.0 all-gather.11.cloned.1.call-done
  561.1 11.5 convolution_bitcast_fusion.1
  572.6 14.4 %all-gather.15.cloned.1.call-done = bf16[704,1024]{1,0:T(8,128)(2,1)} async-done(((bf16[704,128]{1,0:T(8,128)(2,1)}), bf16[704,1024]{1,0:T(8,128)(2,1)}) %all-gather.15.cloned.1.call-update) | async-done | bytes 1441808 | tf_op jit(solution)/shard_map/all_gather | solution.py:138
  587.0 11.3 fusion.41
  600.8 9.0 convolution_bitcast_fusion.2
  609.9 144.6 %reduce-scatter.16.cloned.1.call-done = f32[512,1024]{1,0:T(8,128)} async-done(((f32[2048,1024]{1,0:T(8,128)}), f32[512,1024]{1,0:T(8,128)}) %reduce-scatter.16.cloned.1.call-update) | async-done | bytes 2097168 | tf_op jit(solution)/shard_map/reduce_scatter | solution.py:204
  754.4 2.9 multiply_reduce_fusion.1
  759.3 81.4 %all-gather.17.cloned.1.call-done = bf16[2048,1024]{1,0:T(8,128)(2,1)} async-done(((bf16[512,1024]{1,0:T(8,128)(2,1)}), bf16[2048,1024]{1,0:T(8,128)(2,1)}) %all-gather.17.cloned.1.call-update) | async-done | bytes 4194320 | tf_op jit(solution)/shard_map/all_gather | solution.py:215
  840.7 3.6 fusion.42
  846.1 153.7 %while.56 = (s32[]{:T(128)}, f32[4,2048,64]{1,2,0:T(8,128)}, f32[4,2048,64]{1,2,0:T(8,128)}, f32[4,2048,64]{1,2,0:T(8,128)}, bf16[4,2048,64]{2,1,0:T(8,128)(2,1)...) while((s32[]{:T(128)}, f32[4,2048,64]{1,2,0:T(8,128)}, ...), condition=%wide.region_16.17_spmd, body=%wide.region_12.16_spmd.sunk | while | flops 684197888 | bytes 42895948 | solution.py:221
  851.1 29.9 %while.58 = (s32[]{:T(128)}, f32[2048,64]{0,1:T(8,128)S(1)}, f32[2048,64]{0,1:T(8,128)S(1)}, f32[4,512,64]{1,2,0:T(8,128)}, s32[4]{0:T(128)S(1)}, /*index=5*/s32...) while((s32[]{:T(128)}, f32[2048,64]{0,1:T(8,128)S(1)}, ...), condition=%wide.region_15.15_spmd.clone, body=%wide.region_13.14_spmd.clone.sunk | while | flops 684197888 | bytes 35539192 | solution.py:113
  889.5 29.9 %while.58 = (s32[]{:T(128)}, f32[2048,64]{0,1:T(8,128)S(1)}, f32[2048,64]{0,1:T(8,128)S(1)}, f32[4,512,64]{1,2,0:T(8,128)}, s32[4]{0:T(128)S(1)}, /*index=5*/s32...) while((s32[]{:T(128)}, f32[2048,64]{0,1:T(8,128)S(1)}, ...), condition=%wide.region_15.15_spmd.clone, body=%wide.region_13.14_spmd.clone.sunk | while | flops 684197888 | bytes 35539192 | solution.py:113
  927.9 29.9 %while.58 = (s32[]{:T(128)}, f32[2048,64]{0,1:T(8,128)S(1)}, f32[2048,64]{0,1:T(8,128)S(1)}, f32[4,512,64]{1,2,0:T(8,128)}, s32[4]{0:T(128)S(1)}, /*index=5*/s32...) while((s32[]{:T(128)}, f32[2048,64]{0,1:T(8,128)S(1)}, ...), condition=%wide.region_15.15_spmd.clone, body=%wide.region_13.14_spmd.clone.sunk | while | flops 684197888 | bytes 35539192 | solution.py:113
  966.4 29.9 %while.58 = (s32[]{:T(128)}, f32[2048,64]{0,1:T(8,128)S(1)}, f32[2048,64]{0,1:T(8,128)S(1)}, f32[4,512,64]{1,2,0:T(8,128)}, s32[4]{0:T(128)S(1)}, /*index=5*/s32...) while((s32[]{:T(128)}, f32[2048,64]{0,1:T(8,128)S(1)}, ...), condition=%wide.region_15.15_spmd.clone, body=%wide.region_13.14_spmd.clone.sunk | while | flops 684197888 | bytes 35539192 | solution.py:113
  999.8 3.8 subtract_convert_fusion.1
  1009.9 7.5 bitcast_convert_fusion
  1018.9 7.4 fusion.56
  1027.6 6.9 convolution_convert_fusion
  1034.6 58.2 %reduce-scatter.18.cloned.1.call-done = bf16[512,1024]{1,0:T(8,128)(2,1)} async-done(((bf16[2048,1024]{1,0:T(8,128)(2,1)}), bf16[512,1024]{1,0:T(8,128)(2,1)}) %reduce-scatter.18.cloned.1.call-update) | async-done | bytes 1048592 | tf_op jit(solution)/shard_map/reduce_scatter | solution.py:233
  1096.0 7.8 fusion.32
  1103.8 11.5 fusion.43
  1116.6 4.6 fusion.75
  1121.2 3.0 copy.77
  1124.2 19.0 %reduce-scatter.20.cloned.1.call-done = f32[3,128,256]{1,2,0:T(8,128)} async-done(((f32[3,1024,256]{1,2,0:T(8,128)}), f32[3,128,256]{1,2,0:T(8,128)}) %reduce-scatter.20.cloned.1.call-update) | async-done | bytes 393232 | tf_op jit(solution)/shard_map/reduce_scatter | solution.py:247
  1145.1 77.2 %reduce-scatter.14.cloned.1.call-done = bf16[512,1024]{1,0:T(8,128)(2,1)} async-done(((bf16[2048,1024]{1,0:T(8,128)(2,1)}), bf16[512,1024]{1,0:T(8,128)(2,1)}) %reduce-scatter.14.cloned.1.call-update) | async-done | bytes 1048592 | tf_op jit(solution)/shard_map/reduce_scatter | solution.py:176
  1222.3 4.3 fusion.48
  1226.5 33.7 %reduce-scatter.28.cloned.1.call-done = f32[128,2]{1,0:T(8,128)} async-done(((f32[1024,2]{1,0:T(8,128)}), f32[128,2]{1,0:T(8,128)}) %reduce-scatter.28.cloned.1.call-update) | async-done | bytes 1040
  1261.1 12.2 psum.7
  1273.3 35.7 %reduce-scatter.26.cloned.1.call-done = f32[704,128]{1,0:T(8,128)} async-done(((f32[704,1024]{1,0:T(8,128)}), f32[704,128]{1,0:T(8,128)}) %reduce-scatter.26.cloned.1.call-update) | async-done | bytes 360464 | tf_op jit(solution)/shard_map/reduce_scatter | solution.py:250
  1309.1 63.3 %reduce-scatter.24.cloned.1.call-done = f32[2,128,704]{1,2,0:T(8,128)} async-done(((f32[2,1024,704]{1,2,0:T(8,128)}), f32[2,128,704]{1,2,0:T(8,128)}) %reduce-scatter.24.cloned.1.call-update) | async-done | bytes 720912 | tf_op jit(solution)/shard_map/reduce_scatter | solution.py:249
  1372.4 39.6 %reduce-scatter.22.cloned.1.call-done = f32[256,128]{1,0:T(8,128)} async-done(((f32[256,1024]{1,0:T(8,128)}), f32[256,128]{1,0:T(8,128)}) %reduce-scatter.22.cloned.1.call-update) | async-done | bytes 131088 | tf_op jit(solution)/shard_map/reduce_scatter | solution.py:248
  (540 shorter events, 280.0 us)
Async XLA Ops:
  7.2 18.9 %copy-start.18 = (f32[256,128]{1,0:T(8,128)S(1)}, f32[256,128]{1,0:T(8,128)}, u32[]{:S(2)}) copy-start(f32[256,128]{1,0:T(8,128)} %param.20) | copy-start | bytes 393220
  7.2 18.9 %copy-start.13 = (bf16[2048,256]{1,0:T(8,128)(2,1)S(1)}, bf16[2048,256]{1,0:T(8,128)(2,1)}, u32[]{:S(2)}) copy-start(bf16[2048,256]{1,0:T(8,128)(2,1)} %param.18) | copy-start | bytes 3145732
  7.2 34.4 %all-gather.9.cloned.1.call-start = ((), (), s32[]{:S(2)}) async-start(), calls=%async_computation.10 | async-start | bytes 1769472 | tf_op jit(solution)/shard_map/all_gather | solution.py:135
  9.2 114.3 %all-gather.7.cloned.1.call-start = ((), (), s32[]{:S(2)}) async-start(), calls=%async_computation.9 | async-start | bytes 5242880 | tf_op jit(solution)/shard_map/all_gather | solution.py:146
  21.6 0.6 copy-start.25
  22.2 0.6 copy-start.21
  25.3 387.7 %reduce-scatter.12.cloned.1.call-start = ((), (), s32[]{:S(2)}) async-start(), calls=%async_computation.11 | async-start | bytes 10485760 | tf_op jit(solution)/shard_map/reduce_scatter | solution.py:160
  41.6 88.4 %copy-start.9 = (f32[2048,32]{0,1:T(8,128)}, f32[2048,32]{0,1:T(8,128)S(1)}, u32[]{:S(2)}) copy-start(f32[2048,32]{0,1:T(8,128)S(1)} %get-tuple-element.429) | copy-start | bytes 786436
  263.1 6.7 copy-start.4
  269.8 1.1 copy-start.16
  269.8 143.2 %copy-start.2 = (bf16[512,1024]{1,0:T(8,128)(2,1)S(1)}, bf16[512,1024]{1,0:T(8,128)(2,1)}, u32[]{:S(2)}) copy-start(bf16[512,1024]{1,0:T(8,128)(2,1)} %param.17) | copy-start | bytes 3145732
  269.8 277.2 %all-gather.13.cloned.1.call-start = ((), (), s32[]{:S(2)}) async-start(), calls=%async_computation.13 | async-start | bytes 3244032 | tf_op jit(solution)/shard_map/all_gather | solution.py:137
  271.7 143.3 %copy-start.19 = (f32[1,1024]{1,0:T(1,128)S(1)}, f32[1,1024]{1,0:T(1,128)}, u32[]{:S(2)}) copy-start(f32[1,1024]{1,0:T(1,128)} %get-tuple-element.425) | copy-start | bytes 12292
  271.7 289.3 %all-gather.11.cloned.1.call-start = ((), (), s32[]{:S(2)}) async-start(), calls=%async_computation.12 | async-start | bytes 5242880 | tf_op jit(solution)/shard_map/all_gather | solution.py:168
  414.9 342.4 %copy-start = (f32[512,1024]{1,0:T(8,128)}, f32[512,1024]{1,0:T(8,128)S(1)}, u32[]{:S(2)}) copy-start(f32[512,1024]{1,0:T(8,128)S(1)} %get-tuple-element.395) | copy-start | bytes 6291460
  414.9 2.0 copy-start.6
  414.9 75.8 %copy-start.17 = (f32[704,128]{1,0:T(8,128)S(1)}, f32[704,128]{1,0:T(8,128)}, u32[]{:S(2)}) copy-start(f32[704,128]{1,0:T(8,128)} %param.22) | copy-start | bytes 1081348
  415.0 342.4 %copy-start.23 = (f32[512]{0:T(512)}, f32[512]{0:T(512)S(1)}, u32[]{:S(2)}) copy-start(f32[512]{0:T(512)S(1)} %add_rsqrt_fusion) | copy-start | bytes 6148
  416.2 170.7 %all-gather.15.cloned.1.call-start = ((), (), s32[]{:S(2)}) async-start(), calls=%async_computation.14 | async-start | bytes 1622016 | tf_op jit(solution)/shard_map/all_gather | solution.py:138
  416.9 26.5 %collective-permute-start = (bf16[512,1024]{1,0:T(8,128)(2,1)S(1)}, bf16[512,1024]{1,0:T(8,128)(2,1)S(1)}, u32[]{:S(2)}, u32[]{:S(2)}) collective-permute-start(bf16[512,1024]{1,0:T(8,128)(2,1)S(1)} %copy-done.6), channel_id=1, source_target_pairs={{0,1},{1,2},{2,3},{3,0},{4,5},{5,6},{6,7},{7,4},{8,9},{9,10},{10,1... | collective-permute-start | bytes 3145736 | tf_op jit(solution)/shard_map/ppermute | solution.py:193
  443.5 1.0 copy-start.7
  444.5 36.6 %collective-permute-start.1 = (bf16[512,1024]{1,0:T(8,128)(2,1)S(1)}, bf16[512,1024]{1,0:T(8,128)(2,1)}, u32[]{:S(2)}, u32[]{:S(2)}) collective-permute-start(bf16[512,1024]{1,0:T(8,128)(2,1)S(1)} %collective-permute-done), channel_id=1, source_target_pairs={{0,1},{1,2},{2,3},{3,0},{4,5},{5,6},{6,7},{7,4},{8,9},{9,10},{10,1... | collective-permute-start | bytes 3145736 | tf_op jit(solution)/shard_map/ppermute | solution.py:193
  481.1 52.7 %collective-permute-start.2 = (bf16[512,1024]{1,0:T(8,128)(2,1)}, bf16[512,1024]{1,0:T(8,128)(2,1)}, u32[]{:S(2)}, u32[]{:S(2)}) collective-permute-start(bf16[512,1024]{1,0:T(8,128)(2,1)} %collective-permute-done.1), channel_id=1, source_target_pairs={{0,1},{1,2},{2,3},{3,0},{4,5},{5,6},{6,7},{7,4},{8,9},{9,10},{10,1... | collective-permute-start | bytes 3145736 | tf_op jit(solution)/shard_map/ppermute | solution.py:193
  491.5 262.9 %reduce-scatter.16.cloned.1.call-start = ((), (), s32[]{:S(2)}) async-start(), calls=%async_computation.16 | async-start | bytes 10485760 | tf_op jit(solution)/shard_map/reduce_scatter | solution.py:204
  491.6 46.8 %copy-start.8 = (bf16[512,1024]{1,0:T(8,128)(2,1)S(1)}, bf16[512,1024]{1,0:T(8,128)(2,1)}, u32[]{:S(2)}) copy-start(bf16[512,1024]{1,0:T(8,128)(2,1)} %copy-done.7) | copy-start | bytes 3145732
  587.0 13.9 copy-start.30
  598.3 1.6 copy-start.32
  598.3 2.5 copy-start.33
  609.8 230.9 %all-gather.17.cloned.1.call-start = ((), (), s32[]{:S(2)}) async-start(), calls=%async_computation.17 | async-start | bytes 5242880 | tf_op jit(solution)/shard_map/all_gather | solution.py:215
  754.4 2.9 copy-start.5
  757.4 1.6 copy-start.27
  759.0 333.8 %reduce-scatter.18.cloned.1.call-start = ((), (), s32[]{:S(2)}) async-start(), calls=%async_computation.18 | async-start | bytes 5242880 | tf_op jit(solution)/shard_map/reduce_scatter | solution.py:233
  846.1 153.7 %copy-start.10 = (f32[2048,32]{0,1:T(8,128)S(1)}, f32[2048,32]{0,1:T(8,128)}, u32[]{:S(2)}) copy-start(f32[2048,32]{0,1:T(8,128)} %copy-done.9) | copy-start | bytes 786436
  1003.8 3.9 copy-start.11
  1017.3 1.2 copy-start.14
  1017.3 1.5 copy-start.15
  1017.4 125.8 %reduce-scatter.20.cloned.1.call-start = ((), (), s32[]{:S(2)}) async-start(), calls=%async_computation.19 | async-start | bytes 3538944 | tf_op jit(solution)/shard_map/reduce_scatter | solution.py:247
  1026.2 1.4 copy-start.31
  1026.2 196.0 %reduce-scatter.14.cloned.1.call-start = ((), (), s32[]{:S(2)}) async-start(), calls=%async_computation.15 | async-start | bytes 5242880 | tf_op jit(solution)/shard_map/reduce_scatter | solution.py:176
  1034.5 58.3 %copy-start.3 = (bf16[512,1024]{1,0:T(8,128)(2,1)S(1)}, bf16[512,1024]{1,0:T(8,128)(2,1)}, u32[]{:S(2)}) copy-start(bf16[512,1024]{1,0:T(8,128)(2,1)} %param.17) | copy-start | bytes 3145732
  1034.5 58.3 %copy-start.22 = (f32[1,1024]{1,0:T(1,128)S(1)}, f32[1,1024]{1,0:T(1,128)}, u32[]{:S(2)}) copy-start(f32[1,1024]{1,0:T(1,128)} %copy-done.21) | copy-start | bytes 12292
  1034.5 58.3 %copy-start.26 = (f32[512]{0:T(512)S(1)}, f32[512]{0:T(512)}, u32[]{:S(2)}) copy-start(f32[512]{0:T(512)} %copy-done.25) | copy-start | bytes 6148
  1034.5 60.3 %copy-start.29 = (f32[1024]{0:T(1024)S(1)}, f32[1024]{0:T(1024)}, u32[]{:S(2)}) copy-start(f32[1024]{0:T(1024)} %get-tuple-element.318) | copy-start | bytes 12292
  1034.5 225.7 %reduce-scatter.28.cloned.1.call-start = ((), (), s32[]{:S(2)}) async-start(), calls=%async_computation.23 | async-start | bytes 589824
  1095.9 213.1 %reduce-scatter.26.cloned.1.call-start = ((), (), s32[]{:S(2)}) async-start(), calls=%async_computation.22 | async-start | bytes 3244032 | tf_op jit(solution)/shard_map/reduce_scatter | solution.py:250
  1103.8 268.6 %reduce-scatter.24.cloned.1.call-start = ((), (), s32[]{:S(2)}) async-start(), calls=%async_computation.21 | async-start | bytes 6488064 | tf_op jit(solution)/shard_map/reduce_scatter | solution.py:249
  1115.3 1.2 copy-start.12
  1115.4 296.6 %reduce-scatter.22.cloned.1.call-start = ((), (), s32[]{:S(2)}) async-start(), calls=%async_computation.20 | async-start | bytes 1179648 | tf_op jit(solution)/shard_map/reduce_scatter | solution.py:248
  1121.2 101.1 %copy-start.1 = (f32[512,1024]{1,0:T(8,128)S(1)}, f32[512,1024]{1,0:T(8,128)}, u32[]{:S(2)}) copy-start(f32[512,1024]{1,0:T(8,128)} %copy-done) | copy-start | bytes 6291460
  1121.2 101.1 %copy-start.20 = (f32[1,1024]{1,0:T(1,128)S(1)}, f32[1,1024]{1,0:T(1,128)}, u32[]{:S(2)}) copy-start(f32[1,1024]{1,0:T(1,128)} %get-tuple-element.425) | copy-start | bytes 12292
  1121.2 101.1 %copy-start.24 = (f32[512]{0:T(512)S(1)}, f32[512]{0:T(512)}, u32[]{:S(2)}) copy-start(f32[512]{0:T(512)} %copy-done.23) | copy-start | bytes 6148
  1121.2 101.1 %copy-start.28 = (f32[512]{0:T(512)S(1)}, f32[512]{0:T(512)}, u32[]{:S(2)}) copy-start(f32[512]{0:T(512)} %copy-done.27) | copy-start | bytes 6148
Sparse Core Ops, SparseCore 0:
  10.5 30.0 all-gather.8
  42.7 80.6 all-gather.6
  270.0 142.9 reduce-scatter.11
  415.3 32.3 all-gather.12
  449.7 111.3 all-gather.10
  563.4 23.5 all-gather.14
  609.9 144.4 reduce-scatter.15
  759.2 81.4 all-gather.16
  1017.5 75.2 reduce-scatter.17
  1096.4 46.7 reduce-scatter.19
  1145.5 76.7 reduce-scatter.13
  1225.5 34.6 reduce-scatter.27
  1264.2 44.8 reduce-scatter.25
  1313.3 59.0 reduce-scatter.23
  1376.0 35.9 reduce-scatter.21
